TPU v7x, 256 devices: a whole 4x4x8 slice. The times are simulated.
256 devices in a mesh: lang: 4 (over x_hi, core), blk: 64 (over x_lo, z, y).
Axes of the slice: x: 4 (x_hi: 2, x_lo: 2; x = x_hi * 2 + x_lo), y: 4, z: 8, core: 2. Of those that a mesh axis runs over, the one named last changes fastest.
Arguments:
- fisher: bfloat16 [8, 4096, 16384], P('lang', None, 'blk'), may hold values from 0.049804688 to 5
- factor_left: bfloat16 [8, 4096, 64], P('lang', 'blk'), may hold values from -6 to 6
- factor_right: bfloat16 [8, 64, 16384], P('lang', None, 'blk'), may hold values from -0.75 to 0.75
- base_weight: bfloat16 [4096, 16384], P(('lang', 'blk')), may hold values from -3 to 3
Outputs:
- merged: bfloat16 [4096, 16384], P(('lang', 'blk'))
All inputs are finite; a program needn't handle non-finite values.
Results may differ from a plain program's by a relative error of at most 0.0011.
Values may be sent and summed in bfloat16 or wider, within the bound.
A program may use at most 128 MiB of HBM per device.

v0:
```python
import jax
import jax.numpy as jnp
from jax import lax
from jax.sharding import PartitionSpec as P


def weighted_sums(fisher_part, change):
    weight_wide = fisher_part.astype(jnp.float32)
    return (jnp.sum(weight_wide * change, axis=0), jnp.sum(weight_wide, axis=0))


def shards(fisher, factor_left, factor_right, base_weight):
    lang_count = lax.axis_size("lang")
    blk_count = lax.axis_size("blk")
    local_langs, full_rows, columns = fisher.shape
    row_count = base_weight.shape[0]
    change = jnp.einsum(
        "lir,lrc->lic",
        lax.all_gather(factor_left, "blk", axis=1, tiled=True),
        factor_right,
        preferred_element_type=jnp.float32,
    )
    weighted, totals = weighted_sums(fisher, change)
    weighted = weighted.reshape(lang_count, blk_count, row_count, columns)
    totals = totals.reshape(lang_count, blk_count, row_count, columns)
    moved = (
        lax.all_to_all(weighted, "blk", split_axis=1, concat_axis=3, tiled=True),
        lax.all_to_all(totals, "blk", split_axis=1, concat_axis=3, tiled=True),
    )
    weighted, totals = (
        lax.psum_scatter(moved[0], "lang", scatter_dimension=0, tiled=True),
        lax.psum_scatter(moved[1], "lang", scatter_dimension=0, tiled=True),
    )
    weighted = weighted.reshape(row_count, columns * blk_count)
    totals = totals.reshape(row_count, columns * blk_count)
    return (base_weight.astype(jnp.float32) + weighted / totals).astype(jnp.bfloat16)


def solution(mesh):
    placed = (
        P("lang", None, "blk"),
        P("lang", "blk", None),
        P("lang", None, "blk"),
        P(("lang", "blk"), None),
    )
    return jax.shard_map(
        shards, mesh=mesh, in_specs=placed, out_specs=P(("lang", "blk"), None), check_vma=False
    )
```

profile of v0, /device:TPU:1, one launch (start us, length us, event | category | flops | bytes accessed | tf_op | source)
XLA Modules:
  0.0 475.5 jit_solution(10156410915796598512)
XLA Ops:
  7.4 0.0 copy-start
  7.4 3.5 convert_reduce_fusion
  10.9 2.4 copy.9
  13.3 13.8 %all-to-all-start.1 = ((f32[4,64,16,256]{3,2,0,1:T(8,128)}), f32[4,64,16,256]{3,2,0,1:T(8,128)}, u32[]{:S(2)}, u32[]{:S(2)}) async-start(f32[4,64,16,256]{3,2,0,1:T(8,128)} %copy.9), calls=%async_computation.2 | async-start | bytes 8388608 | tf_op jit(solution)/shard_map/all_to_all | solution.py:28
  27.1 0.0 all-gather.2.cloned.1.call-start
  27.2 0.7 all-gather.2.cloned.1.call-update
  27.9 0.0 reduce-scatter.5.cloned.1.call-start
  27.9 91.7 %all-to-all-done.1 = f32[4,64,16,256]{3,2,0,1:T(8,128)} async-done(((f32[4,64,16,256]{3,2,0,1:T(8,128)}), f32[4,64,16,256]{3,2,0,1:T(8,128)}, u32[]{:S(2)}, u32[]{:S(2)}) %all-to-all-start.1) | async-done | bytes 4194336 | tf_op jit(solution)/shard_map/all_to_all | solution.py:28
  119.6 4.5 copy.12
  124.2 0.0 reduce-scatter.5.cloned.1.call-update
  124.2 0.0 reduce-scatter.3.cloned.1.call-start
  124.3 178.3 %all-gather.2.cloned.1.call-done = bf16[2,4096,64]{2,1,0:T(8,128)(2,1)} async-done(((bf16[2,64,64]{2,1,0:T(8,128)(2,1)}), bf16[2,4096,64]{2,1,0:T(8,128)(2,1)}) %all-gather.2.cloned.1.call-update) | async-done | bytes 1048592 | tf_op jit(solution)/shard_map/all_gather | solution.py:19
  302.6 0.0 copy-done
  302.6 4.4 fusion
  307.0 0.5 copy.7
  307.5 61.9 %all_to_all.36 = f32[4,64,16,256]{3,2,0,1:T(8,128)S(1)} all-to-all(f32[4,64,16,256]{3,2,0,1:T(8,128)S(1)} %copy.7), channel_id=1, replica_groups=mesh['lang'=4,'blk'=64] {'blk'}, dimensions={1} | all-to-all | bytes 8388608 | tf_op jit(solution)/shard_map/all_to_all | solution.py:27
  369.4 2.4 copy.11
  371.8 0.0 copy-start.1
  371.8 0.0 reduce-scatter.3.cloned.1.call-update
  371.8 0.0 reduce-scatter.5.cloned.1.call-done
  371.8 93.8 %reduce-scatter.3.cloned.1.call-done = f32[1,1,16,16384]{3,2,0,1:T(8,128)} async-done(((f32[4,1,16,16384]{3,2,0,1:T(8,128)}), f32[1,1,16,16384]{3,2,0,1:T(8,128)}) %reduce-scatter.3.cloned.1.call-update) | async-done | bytes 1048592 | tf_op jit(solution)/shard_map/reduce_scatter | solution.py:31
  465.6 0.0 copy-done.1
  465.6 2.5 fusion.1
Async XLA Ops:
  7.4 295.2 %copy-start = (bf16[2,64,256]{2,1,0:T(8,128)(2,1)S(1)}, bf16[2,64,256]{2,1,0:T(8,128)(2,1)}, u32[]{:S(2)}) copy-start(bf16[2,64,256]{2,1,0:T(8,128)(2,1)} %param.6) | copy-start | bytes 196612
  13.3 106.4 %all-to-all-start.1 = ((f32[4,64,16,256]{3,2,0,1:T(8,128)}), f32[4,64,16,256]{3,2,0,1:T(8,128)}, u32[]{:S(2)}, u32[]{:S(2)}) async-start(f32[4,64,16,256]{3,2,0,1:T(8,128)} %copy.9), calls=%async_computation.2 | async-start | bytes 8388608 | tf_op jit(solution)/shard_map/all_to_all | solution.py:28
  27.1 275.4 %all-gather.2.cloned.1.call-start = ((), (), s32[]{:S(2)}) async-start(), calls=%async_computation.4 | async-start | bytes 2129920 | tf_op jit(solution)/shard_map/all_gather | solution.py:19
  27.9 343.9 %reduce-scatter.5.cloned.1.call-start = ((), (), s32[]{:S(2)}) async-start(), calls=%async_computation.6 | async-start | bytes 5242880 | tf_op jit(solution)/shard_map/reduce_scatter | solution.py:32
  124.2 341.4 %reduce-scatter.3.cloned.1.call-start = ((), (), s32[]{:S(2)}) async-start(), calls=%async_computation.5 | async-start | bytes 5242880 | tf_op jit(solution)/shard_map/reduce_scatter | solution.py:31
  371.8 93.8 %copy-start.1 = (bf16[16,16384]{1,0:T(8,128)(2,1)S(1)}, bf16[16,16384]{1,0:T(8,128)(2,1)}, u32[]{:S(2)}) copy-start(bf16[16,16384]{1,0:T(8,128)(2,1)} %param.7) | copy-start | bytes 1572868
Sparse Core Ops, SparseCore 0:
  29.9 272.6 all-gather.1
Sparse Core Ops, SparseCore 1:
  124.3 63.0 reduce-scatter.4
  371.9 93.7 reduce-scatter.2
where the time goes:
time: 476 us
  waiting for transfers between devices  365 us (77%)
  blocking collectives  61.9 us (13%)
  between operations  14.9 us (3%)
  starting transfers between devices  14 us (3%)
  local copies, waits for them, and re-layouts  9.77 us (2%)
  other arithmetic  6 us (1%)
    all_gather x1, waiting for transfers between devices, shards(): lax.all_gather(factor_left, 'blk', axis=1, tiled=True)  178 us
    reduce_scatter x1, waiting for transfers between devices, shards(): lax.psum_scatter(moved[0], 'lang', scatter_dimension=0, tiled=True)  93.8 us
    all_to_all x1, waiting for transfers between devices, shards(): lax.all_to_all(totals, 'blk', split_axis=1, concat_axis=3, tiled=True)  91.7 us
    all_to_all x1, blocking collectives, shards(): lax.all_to_all(weighted, 'blk', split_axis=1, concat_axis=3, tiled=True)  61.9 us
    all_to_all x1, starting transfers between devices, shards(): lax.all_to_all(totals, 'blk', split_axis=1, concat_axis=3, tiled=True)  13.8 us
  transfers between devices with their start and end apart: 4, of which 3 were waited for; matrix products, arithmetic and copies ran while one was open for 2% of the time, Pallas kernels for 0%

commit v1 on v0

--- a/solution.py
+++ b/solution.py
@@ -24,7 +24,12 @@
     weighted = weighted.reshape(lang_count, blk_count, row_count, columns)
     totals = totals.reshape(lang_count, blk_count, row_count, columns)
     moved = (
-        lax.all_to_all(weighted, "blk", split_axis=1, concat_axis=3, tiled=True),
+        jnp.concatenate(
+            lax.all_to_all(
+                jnp.stack(jnp.split(weighted, lax.axis_size("blk"), axis=1)), "blk", 0, 0
+            ),
+            axis=3,
+        ),
         lax.all_to_all(totals, "blk", split_axis=1, concat_axis=3, tiled=True),
     )
     weighted, totals = (

time: 476 us -> 512 us (1.076)
  local copies, waits for them, and re-layouts: 9.77 us -> 51.1 us
  waiting for transfers between devices: 365 us -> 354 us
  blocking collectives: 61.9 us -> 67.3 us
    all_to_all x1, waiting for transfers between devices: 91.7 us -> 0.01 us  [shards(): lax.all_to_all(totals, 'blk', split_axis=1, concat_axis=3, tiled=True)]
    all_gather x1, waiting for transfers between devices: 178 us -> 260 us  [shards(): lax.all_gather(factor_left, 'blk', axis=1, tiled=True)]
    unnamed x4 -> x69, local copies, waits for them, and re-layouts: 0.01 us -> 40.3 us
    reduce_scatter x1, waiting for transfers between devices: 93.8 us -> 58 us  [shards(): lax.psum_scatter(moved[0], 'lang', scatter_dimension=0, tiled=True)]
    reduce_scatter x1, waiting for transfers between devices: 0.03 us -> 35 us  [shards(): lax.psum_scatter(moved[1], 'lang', scatter_dimension=0, tiled=True)]
    all_to_all x1, blocking collectives: 61.9 us -> 67.3 us  [shards(): lax.all_to_all(jnp.stack(jnp.split(weighted, lax.axis_size('blk'), axis=1...]
  transfers between devices with their start and end apart: 4 -> 4, of which waited for: 3 -> 3; matrix products, arithmetic and copies ran while one was open for 2% -> 11% of each run, Pallas kernels for 0% -> 0%
where the time goes in v1:
time: 512 us
  waiting for transfers between devices  354 us (69%)
  blocking collectives  67.3 us (13%)
  local copies, waits for them, and re-layouts  51.1 us (10%)
  between operations  14.9 us (3%)
  starting transfers between devices  13.9 us (3%)
  other arithmetic  6 us (1%)
    all_gather x1, waiting for transfers between devices, shards(): lax.all_gather(factor_left, 'blk', axis=1, tiled=True)  260 us
    all_to_all x1, blocking collectives, shards(): lax.all_to_all(jnp.stack(jnp.split(weighted, lax.axis_size('blk'), axis=1...  67.3 us
    reduce_scatter x1, waiting for transfers between devices, shards(): lax.psum_scatter(moved[0], 'lang', scatter_dimension=0, tiled=True)  58 us
    unnamed x69, local copies, waits for them, and re-layouts  40.3 us
    reduce_scatter x1, waiting for transfers between devices, shards(): lax.psum_scatter(moved[1], 'lang', scatter_dimension=0, tiled=True)  35 us
    all_to_all x1, starting transfers between devices, shards(): lax.all_to_all(totals, 'blk', split_axis=1, concat_axis=3, tiled=True)  13.8 us
  transfers between devices with their start and end apart: 4, of which 3 were waited for; matrix products, arithmetic and copies ran while one was open for 11% of the time, Pallas kernels for 0%

profile of v1, /device:TPU:1, one launch (start us, length us, event | category | flops | bytes accessed | tf_op | source)
XLA Modules:
  0.0 511.6 jit_solution(11531673330368168451)
XLA Ops:
  7.4 0.7 all-gather.2.cloned.1.call-update
  8.1 3.5 convert_reduce_fusion
  11.6 2.4 copy.260
  14.0 13.8 %all-to-all-start.1 = ((f32[4,64,16,256]{3,2,0,1:T(8,128)}), f32[4,64,16,256]{3,2,0,1:T(8,128)}, u32[]{:S(2)}, u32[]{:S(2)}) async-start(f32[4,64,16,256]{3,2,0,1:T(8,128)} %copy.260), calls=%async_computation.2 | async-start | bytes 8388608 | tf_op jit(solution)/shard_map/all_to_all | solution.py:33
  27.9 260.2 %all-gather.2.cloned.1.call-done = bf16[2,4096,64]{2,1,0:T(8,128)(2,1)} async-done(((bf16[2,64,64]{2,1,0:T(8,128)(2,1)}), bf16[2,4096,64]{2,1,0:T(8,128)(2,1)}) %all-gather.2.cloned.1.call-update) | async-done | bytes 1048592 | tf_op jit(solution)/shard_map/all_gather | solution.py:19
  288.1 4.4 fusion
  292.5 0.7 constant_dynamic-update-slice_fusion.63
  293.2 1.1 constant_dynamic-update-slice_fusion.62
  295.0 0.6 constant_dynamic-update-slice_fusion.60
  295.6 0.6 constant_dynamic-update-slice_fusion.59
  296.2 0.6 constant_dynamic-update-slice_fusion.58
  296.9 0.6 constant_dynamic-update-slice_fusion.57
  297.5 0.6 constant_dynamic-update-slice_fusion.56
  298.2 0.6 constant_dynamic-update-slice_fusion.55
  298.8 0.6 constant_dynamic-update-slice_fusion.54
  299.4 0.6 constant_dynamic-update-slice_fusion.53
  300.1 0.6 constant_dynamic-update-slice_fusion.52
  300.7 0.6 constant_dynamic-update-slice_fusion.51
  301.3 0.6 constant_dynamic-update-slice_fusion.50
  301.9 0.6 constant_dynamic-update-slice_fusion.49
  302.6 0.6 constant_dynamic-update-slice_fusion.48
  303.2 0.6 constant_dynamic-update-slice_fusion.47
  304.5 0.6 constant_dynamic-update-slice_fusion.45
  305.1 0.6 constant_dynamic-update-slice_fusion.44
  306.4 0.6 constant_dynamic-update-slice_fusion.42
  307.0 0.6 constant_dynamic-update-slice_fusion.41
  307.6 0.6 constant_dynamic-update-slice_fusion.40
  308.3 0.6 constant_dynamic-update-slice_fusion.39
  308.9 0.6 constant_dynamic-update-slice_fusion.38
  310.2 0.6 constant_dynamic-update-slice_fusion.36
  310.8 0.6 constant_dynamic-update-slice_fusion.35
  311.4 0.6 constant_dynamic-update-slice_fusion.34
  312.1 0.6 constant_dynamic-update-slice_fusion.33
  313.9 0.6 constant_dynamic-update-slice_fusion.30
  314.6 0.6 constant_dynamic-update-slice_fusion.29
  315.2 0.6 constant_dynamic-update-slice_fusion.28
  315.9 0.6 constant_dynamic-update-slice_fusion.27
  316.5 0.6 constant_dynamic-update-slice_fusion.26
  317.1 0.6 constant_dynamic-update-slice_fusion.25
  317.8 0.6 constant_dynamic-update-slice_fusion.24
  318.4 0.6 constant_dynamic-update-slice_fusion.23
  319.0 0.6 constant_dynamic-update-slice_fusion.22
  319.7 0.6 constant_dynamic-update-slice_fusion.21
  320.9 0.6 constant_dynamic-update-slice_fusion.19
  321.5 0.6 constant_dynamic-update-slice_fusion.18
  322.2 0.6 constant_dynamic-update-slice_fusion.17
  322.8 0.6 constant_dynamic-update-slice_fusion.16
  324.1 0.6 constant_dynamic-update-slice_fusion.14
  324.7 0.6 constant_dynamic-update-slice_fusion.13
  325.3 0.6 constant_dynamic-update-slice_fusion.12
  326.0 0.6 constant_dynamic-update-slice_fusion.11
  326.6 0.6 constant_dynamic-update-slice_fusion.10
  327.8 0.6 constant_dynamic-update-slice_fusion.8
  329.1 0.6 constant_dynamic-update-slice_fusion.6
  329.7 0.6 constant_dynamic-update-slice_fusion.5
  331.6 0.6 constant_dynamic-update-slice_fusion.2
  332.2 0.6 constant_dynamic-update-slice_fusion.1
  332.9 4.6 copy.326
  337.5 1.5 constant_dynamic-update-slice_fusion
  339.0 67.3 %all_to_all.23 = f32[64,4,1,16,256]{4,3,1,2,0:T(8,128)S(1)} all-to-all(f32[64,4,1,16,256]{4,3,1,2,0:T(8,128)} %constant_dynamic-update-slice_fusion), channel_id=1, replica_groups=mesh['lang'=4,'blk'=64] {'blk'}, dimensions={0} | all-to-all | bytes 8388608 | tf_op jit(solution)/shard_map/all_to_all | solution.py:28
  406.2 2.3 copy.325
  408.6 35.0 %reduce-scatter.5.cloned.1.call-done = f32[1,1,16,16384]{3,2,0,1:T(8,128)} async-done(((f32[4,1,16,16384]{3,2,0,1:T(8,128)}), f32[1,1,16,16384]{3,2,0,1:T(8,128)}) %reduce-scatter.5.cloned.1.call-update) | async-done | bytes 1048592 | tf_op jit(solution)/shard_map/reduce_scatter | solution.py:37
  443.6 58.0 %reduce-scatter.3.cloned.1.call-done = f32[1,1,16,16384]{3,2,0,1:T(8,128)} async-done(((f32[4,1,16,16384]{3,2,0,1:T(8,128)}), f32[1,1,16,16384]{3,2,0,1:T(8,128)}) %reduce-scatter.3.cloned.1.call-update) | async-done | bytes 1048592 | tf_op jit(solution)/shard_map/reduce_scatter | solution.py:36
  501.6 2.5 fusion.1
  (24 shorter events, 7.6 us)
Async XLA Ops:
  7.4 280.7 %copy-start = (bf16[2,64,256]{2,1,0:T(8,128)(2,1)S(1)}, bf16[2,64,256]{2,1,0:T(8,128)(2,1)}, u32[]{:S(2)}) copy-start(bf16[2,64,256]{2,1,0:T(8,128)(2,1)} %param.6) | copy-start | bytes 196612
  7.4 280.7 %all-gather.2.cloned.1.call-start = ((), (), s32[]{:S(2)}) async-start(), calls=%async_computation.4 | async-start | bytes 2129920 | tf_op jit(solution)/shard_map/all_gather | solution.py:19
  14.0 318.9 %all-to-all-start.1 = ((f32[4,64,16,256]{3,2,0,1:T(8,128)}), f32[4,64,16,256]{3,2,0,1:T(8,128)}, u32[]{:S(2)}, u32[]{:S(2)}) async-start(f32[4,64,16,256]{3,2,0,1:T(8,128)} %copy.260), calls=%async_computation.2 | async-start | bytes 8388608 | tf_op jit(solution)/shard_map/all_to_all | solution.py:33
  27.9 415.7 %reduce-scatter.5.cloned.1.call-start = ((), (), s32[]{:S(2)}) async-start(), calls=%async_computation.6 | async-start | bytes 5242880 | tf_op jit(solution)/shard_map/reduce_scatter | solution.py:37
  292.5 39.7 %copy-start.1 = (f32[4096,256]{1,0:T(8,128)}, f32[4096,256]{1,0:T(8,128)S(1)}, u32[]{:S(2)}) copy-start(f32[4096,256]{1,0:T(8,128)S(1)} %fusion) | copy-start | bytes 12582916
  337.5 164.2 %reduce-scatter.3.cloned.1.call-start = ((), (), s32[]{:S(2)}) async-start(), calls=%async_computation.5 | async-start | bytes 5242880 | tf_op jit(solution)/shard_map/reduce_scatter | solution.py:36
  408.6 93.1 %copy-start.2 = (bf16[16,16384]{1,0:T(8,128)(2,1)S(1)}, bf16[16,16384]{1,0:T(8,128)(2,1)}, u32[]{:S(2)}) copy-start(bf16[16,16384]{1,0:T(8,128)(2,1)} %param.7) | copy-start | bytes 1572868
Sparse Core Ops, SparseCore 0:
  10.1 277.9 all-gather.1
Sparse Core Ops, SparseCore 1:
  337.5 106.0 reduce-scatter.4
  446.5 55.1 reduce-scatter.2
